TPU v7x, 128 devices: a whole 4x4x4 slice. The times are simulated.
128 devices in a mesh: sub: 32 (over x, y, core), rep: 4 (over z).
Axes of the slice: x: 4, y: 4, z: 4, core: 2. Of those that a mesh axis runs over, the one named last changes fastest.
Arguments:
- loads: bfloat16 [256, 256, 1024], P('sub', 'rep'), may hold values from -6 to 6
- operators: bfloat16 [256, 1024, 1024], P('sub'), may hold values from -0.1875 to 0.1875
- owner: int32 [2048, 1], P('sub'), may hold values from 0 to 31; in each aligned block of 64 rows (0 to 63, 64 to 127, ...) at most 4 rows name the same one
- dual_block: int32 [2048], P('sub'), may hold values from 0 to 15
- scale_index: int32 [65536], P('sub'), may hold values from 0 to 3
- basis: bfloat16 [65536, 1024], P('sub'), may hold values from -0.0234375 to 0.0234375
- coarse: bfloat16 [1024, 1024], replicated, may hold values from -1.5 to 1.5
Outputs:
- start: float32 [256, 65536], P('rep', 'sub')
- resid: float32 [256, 65536], P('rep', 'sub')
Inputs may be any that keep to these rules, and one draw needn't show every extreme that they name: Among the blocks of the subdomains of one index of sub (aligned blocks of 64 rows), no owner is named more than 4 times, a bound that some block reaches.
All inputs are finite; a program needn't handle non-finite values.
Results may differ from a plain program's by a relative error of at most 0.0075.
Values may be sent and summed in bfloat16 or wider, within the bound.
No kernel may reach another device: no remote copies, remote signals or barrier semaphores. Data moves between devices by JAX's collectives and lax.ppermute only.
A program may use at most 128 MiB of HBM per device.

v0:
```python
import jax
import jax.numpy as jnp
from jax import lax
from jax.sharding import PartitionSpec as P

BLK = 128


def apply_local(inputs, operators):
    return jnp.einsum("skl,slm->skm", inputs, operators, preferred_element_type=jnp.float32).astype(
        jnp.bfloat16
    )


def make_blocks(values, width):
    count, columns, local = values.shape
    return (
        values.reshape(count, columns, local // width, width)
        .transpose(0, 2, 1, 3)
        .reshape(-1, columns, width)
    )


def from_blocks(blocks, count):
    total, columns, width = blocks.shape
    per_sub = total // count
    return (
        blocks.reshape(count, per_sub, columns, width)
        .transpose(0, 2, 1, 3)
        .reshape(count, columns, per_sub * width)
    )


def pack_slots(blocks, dests, ranks, peers, slots):
    columns, width = (blocks.shape[1], blocks.shape[2])
    return jnp.zeros((peers, slots, columns, width), jnp.bfloat16).at[dests, ranks].set(blocks)


def accumulate(received, got_ids, own_blocks, weight):
    columns, width = (received.shape[2], received.shape[3])
    flat = received.reshape(-1, columns, width).astype(jnp.float32)
    total = jnp.zeros((own_blocks, columns, width), jnp.float32).at[got_ids.reshape(-1)].add(flat)
    return total.transpose(1, 0, 2).reshape(columns, own_blocks * width) * weight[None, :]


def per_device(loads, operators, owner, dual_block, scale_index, basis, coarse):
    sub_count = loads.shape[0]
    width = BLK
    peers = lax.axis_size("sub")
    dests = owner[:, 0]
    nblocks = dests.shape[0]
    slots = max(2, 2 * nblocks // peers)
    own_blocks = basis.shape[0] // width
    positions = jnp.arange(nblocks, dtype=jnp.int32)
    earlier = positions[None, :] < positions[:, None]
    same = dests[None, :] == dests[:, None]
    ranks = jnp.sum(jnp.logical_and(earlier, same), axis=1)
    weight = 1.0 / (1.0 + scale_index.astype(jnp.float32))
    terms = apply_local(loads, operators)
    packed = pack_slots(make_blocks(terms, width), dests, ranks, peers, slots)
    id_slots = jnp.zeros((peers, slots), jnp.int32).at[dests, ranks].set(dual_block)
    received, got_ids = (
        lax.all_to_all(packed, "sub", split_axis=0, concat_axis=0, tiled=True),
        lax.all_to_all(id_slots, "sub", split_axis=0, concat_axis=0, tiled=True),
    )
    dual = accumulate(received, got_ids, own_blocks, weight)
    coeff = jnp.dot(dual.astype(jnp.bfloat16), basis, preferred_element_type=jnp.float32)
    summed = lax.psum(coeff, "sub")
    solved = jnp.dot(
        summed.astype(jnp.bfloat16), coarse, preferred_element_type=jnp.float32
    ).astype(jnp.bfloat16)
    start = lax.dot_general(
        solved, basis, (((1,), (1,)), ((), ())), preferred_element_type=jnp.float32
    )
    columns = start.shape[0]
    start_blocks = start.astype(jnp.bfloat16).reshape(columns, own_blocks, width).transpose(1, 0, 2)
    requested = start_blocks[got_ids]
    returned = lax.all_to_all(requested, "sub", split_axis=0, concat_axis=0, tiled=True)
    picked = returned[dests, ranks]
    local = from_blocks(picked, sub_count)
    again = apply_local(local, operators)
    received_again = lax.all_to_all(
        pack_slots(make_blocks(again, width), dests, ranks, peers, slots),
        "sub",
        split_axis=0,
        concat_axis=0,
        tiled=True,
    )
    applied = accumulate(received_again, got_ids, own_blocks, weight)
    return (start, dual - applied)


def solution(mesh):
    return jax.shard_map(
        per_device,
        mesh=mesh,
        in_specs=(
            P("sub", "rep", None),
            P("sub", None, None),
            P("sub", None),
            P("sub"),
            P("sub"),
            P("sub", None),
            P(),
        ),
        out_specs=(P("rep", "sub"), P("rep", "sub")),
        check_vma=False,
    )
```

profile of v0, /device:TPU:1, one launch (start us, length us, event | category | flops | bytes accessed | tf_op | source)
XLA Modules:
  0.0 336.0 jit_solution(8166071477639882503)
XLA Ops:
  0.6 1.0 convert_reduce_fusion
  1.6 0.7 fusion.15
  2.3 5.7 %scatter_fusion = s32[32,4]{0,1:T(4,128)S(1)} fusion(s32[32,4]{0,1:T(4,128)S(1)} %broadcast.75, s32[64]{0:T(128)S(1)} %get-tuple-element.2, s32[64]{0:T(128)} %param.10), kind=kCustom, calls=%fused_computation.2 | custom fusion | bytes 1280 | tf_op jit(solution)/shard_map/scatter | solution.py:61
  8.1 0.7 copy.33
  8.8 8.6 %all-to-all-start = ((s32[32,1,4]{2,1,0:T(1,128)}), s32[32,1,4]{2,1,0:T(1,128)S(1)}, u32[]{:S(2)}, u32[]{:S(2)}) async-start(s32[32,1,4]{2,1,0:T(1,128)} %copy.33), calls=%async_computation | async-start | bytes 32768 | tf_op jit(solution)/shard_map/all_to_all | solution.py:64
  17.4 9.1 %fusion = bf16[8,8,8,8,128]{4,3,2,1,0:T(8,128)(2,1)S(1)} fusion(bf16[8,64,1024]{2,1,0:T(8,128)(2,1)} %param.7, bf16[8,1024,1024]{2,1,0:T(8,128)(2,1)} %param.8), kind=kOutput, calls=%fused_computation.11 | convolution fusion | flops 1074266112 | bytes 18874368 | tf_op jit(solution)/shard_map/skl,slm->skm/dot_general | solution.py:10
  26.5 0.3 copy.63
  26.8 1.9 broadcast.81.clone
  28.7 8.9 %scatter_fusion.1 = bf16[32,4,64,128]{3,2,1,0:T(8,128)(2,1)} fusion(bf16[32,4,64,128]{3,2,1,0:T(8,128)(2,1)} %broadcast.81.clone, s32[64]{0:T(128)S(1)} %get-tuple-element.2, bf16[64,64,128]{2,1,0:T(8,128)(2,1)S(1)} %bitcast.87), kind=kCustom, calls=%fused_computation.3 | custom fusion | bytes 3146240 | tf_op jit(solution)/shard_map/scatter | solution.py:36
  37.5 7.6 %all-to-all-start.1 = ((bf16[32,4,64,128]{3,2,1,0:T(8,128)(2,1)}), bf16[32,4,64,128]{3,2,1,0:T(8,128)(2,1)}, u32[]{:S(2)}, u32[]{:S(2)}) async-start(bf16[32,4,64,128]{3,2,1,0:T(8,128)(2,1)} %scatter_fusion.1), calls=%async_computation.1 | async-start | bytes 4194304 | tf_op jit(solution)/shard_map/all_to_all | solution.py:63
  45.1 0.5 broadcast.184
  45.7 0.7 reduce.3
  46.4 0.1 reshape.115
  46.6 0.1 reshape.129
  46.8 26.7 %all-to-all-done.1 = bf16[32,4,64,128]{3,2,1,0:T(8,128)(2,1)} async-done(((bf16[32,4,64,128]{3,2,1,0:T(8,128)(2,1)}), bf16[32,4,64,128]{3,2,1,0:T(8,128)(2,1)}, u32[]{:S(2)}, u32[]{:S(2)}) %all-to-all-start.1) | async-done | bytes 2097184 | tf_op jit(solution)/shard_map/all_to_all | solution.py:63
  73.5 4.0 %bitcast_convert_fusion.1 = f32[128,64,128]{2,1,0:T(8,128)} fusion(bf16[32,4,64,128]{3,2,1,0:T(8,128)(2,1)} %all-to-all-done.1), kind=kLoop, calls=%fused_computation.8 | loop fusion | flops 1048576 | bytes 6291456 | tf_op jit(solution)/shard_map/convert_element_type | solution.py:41
  77.5 13.5 %scatter_fusion.2 = f32[16,64,128]{2,1,0:T(8,128)S(1)} fusion(f32[16,64,128]{2,1,0:T(8,128)S(1)} %broadcast.74.clone, s32[128]{0:T(128)S(1)} %fusion.14, f32[128,64,128]{2,1,0:T(8,128)} %bitcast_convert_fusion.1), kind=kCustom, calls=%fused_computation.4 | custom fusion | flops 1048576 | bytes 12583424 | tf_op jit(solution)/shard_map/scatter-add | solution.py:42
  91.1 3.0 fusion.7
  94.1 121.1 %all-reduce.1 = bf16[64,1024]{1,0:T(8,128)(2,1)S(1)} all-reduce(f32[64,1024]{1,0:T(8,128)S(1)} %fusion.7), channel_id=1, replica_groups=mesh['sub'=32,'rep'=4] {'sub'}, use_global_device_ids=true, to_apply=%region_4.0 | all-reduce | flops 65536 | bytes 393216 | tf_op jit(solution)/shard_map/psum | solution.py:68
  215.3 4.8 %fusion.2 = f32[64,2048]{1,0:T(8,128)} fusion(bf16[2048,1024]{1,0:T(8,128)(2,1)} %param.12, bf16[1024,1024]{1,0:T(8,128)(2,1)S(1)} %copy-done, bf16[64,1024]{1,0:T(8,128)(2,1)S(1)} %all-reduce.1), kind=kOutput, calls=%fused_computation.14 | convolution fusion | flops 402718720 | bytes 6946816 | tf_op jit(solution)/shard_map/dot_general | solution.py:72
  220.0 1.1 bitcast_bitcast_fusion
  221.1 2.1 gather_fusion
  223.2 38.3 %all_to_all.27 = bf16[32,4,64,128]{3,2,1,0:T(8,128)(2,1)} all-to-all(bf16[32,4,64,128]{3,2,1,0:T(8,128)(2,1)} %bitcast.85), channel_id=1, replica_groups=mesh['sub'=32,'rep'=4] {'sub'}, dimensions={0} | all-to-all | bytes 4194304 | tf_op jit(solution)/shard_map/all_to_all | solution.py:78
  261.5 3.3 gather_fusion.1
  264.8 9.1 %fusion.1 = bf16[8,8,8,8,128]{4,3,2,1,0:T(8,128)(2,1)S(1)} fusion(bf16[8,1024,1024]{2,1,0:T(8,128)(2,1)} %param.8, bf16[8,8,8,8,128]{4,3,2,1,0:T(8,128)(2,1)} %bitcast.88), kind=kOutput, calls=%fused_computation.12 | convolution fusion | flops 1074266112 | bytes 18874368 | tf_op jit(solution)/shard_map/skl,slm->skm/dot_general | solution.py:10
  273.9 1.3 copy.62
  275.2 1.9 broadcast.81
  277.1 9.8 %scatter_fusion.3 = bf16[32,4,64,128]{3,2,1,0:T(8,128)(2,1)} fusion(bf16[32,4,64,128]{3,2,1,0:T(8,128)(2,1)} %broadcast.81, s32[64]{0:T(128)S(1)} %get-tuple-element.2, bf16[64,64,128]{2,1,0:T(8,128)(2,1)} %bitcast.86), kind=kCustom, calls=%fused_computation.5 | custom fusion | bytes 3146240 | tf_op jit(solution)/shard_map/scatter | solution.py:36
  286.9 32.1 %all_to_all.28 = bf16[32,4,64,128]{3,2,1,0:T(8,128)(2,1)S(1)} all-to-all(bf16[32,4,64,128]{3,2,1,0:T(8,128)(2,1)} %scatter_fusion.3), channel_id=1, replica_groups=mesh['sub'=32,'rep'=4] {'sub'}, dimensions={0} | all-to-all | bytes 4194304 | tf_op jit(solution)/shard_map/all_to_all | solution.py:82
  319.0 2.5 bitcast_convert_fusion
  321.6 13.5 %scatter_fusion.4 = f32[16,64,128]{2,1,0:T(8,128)S(1)} fusion(f32[16,64,128]{2,1,0:T(8,128)S(1)} %broadcast.74, s32[128]{0:T(128)S(1)} %fusion.14, f32[128,64,128]{2,1,0:T(8,128)} %bitcast_convert_fusion), kind=kCustom, calls=%fused_computation.6 | custom fusion | flops 1048576 | bytes 12583424 | tf_op jit(solution)/shard_map/scatter-add | solution.py:42
  335.1 0.9 fusion.5
  (14 shorter events, 0.3 us)
Async XLA Ops:
  0.6 214.6 %copy-start = (bf16[1024,1024]{1,0:T(8,128)(2,1)S(1)}, bf16[1024,1024]{1,0:T(8,128)(2,1)}, u32[]{:S(2)}) copy-start(bf16[1024,1024]{1,0:T(8,128)(2,1)} %param.13) | copy-start | bytes 6291460
  8.8 28.8 %all-to-all-start = ((s32[32,1,4]{2,1,0:T(1,128)}), s32[32,1,4]{2,1,0:T(1,128)S(1)}, u32[]{:S(2)}, u32[]{:S(2)}) async-start(s32[32,1,4]{2,1,0:T(1,128)} %copy.33), calls=%async_computation | async-start | bytes 32768 | tf_op jit(solution)/shard_map/all_to_all | solution.py:64
  37.5 7.6 %copy-start.1 = (s32[2048]{0:T(1024)S(1)}, s32[2048]{0:T(1024)}, u32[]{:S(2)}) copy-start(s32[2048]{0:T(1024)} %param.11) | copy-start | bytes 24580
  37.5 35.9 %all-to-all-start.1 = ((bf16[32,4,64,128]{3,2,1,0:T(8,128)(2,1)}), bf16[32,4,64,128]{3,2,1,0:T(8,128)(2,1)}, u32[]{:S(2)}, u32[]{:S(2)}) async-start(bf16[32,4,64,128]{3,2,1,0:T(8,128)(2,1)} %scatter_fusion.1), calls=%async_computation.1 | async-start | bytes 4194304 | tf_op jit(solution)/shard_map/all_to_all | solution.py:63
where the time goes:
time: 338 us; the launch traced here: 336 us
  blocking collectives  192 us (57%)
  other arithmetic  37.9 us (11%)
  local copies, waits for them, and re-layouts  36.8 us (11%)
  waiting for transfers between devices  26.7 us (8%)
  matrix products  26.1 us (8%)
  starting transfers between devices  16.2 us (5%)
    psum x1, blocking collectives, per_device(): summed = lax.psum(coeff, 'sub')  121 us
    all_to_all x1, blocking collectives, per_device(): lax.all_to_all(requested, 'sub', split_axis=0, concat_axis=0, tiled=True)  38.3 us
    all_to_all x1, blocking collectives, per_device(): lax.all_to_all(pack_slots(make_blocks(again, width), dests, ranks, peers,...  32.1 us
    scatter-add x2, other arithmetic, accumulate(): jnp.zeros((own_blocks, columns, width), jnp.float32).at[got_ids.reshape(-1)]  27.1 us
    all_to_all x1, waiting for transfers between devices, per_device(): lax.all_to_all(packed, 'sub', split_axis=0, concat_axis=0, tiled=True)  26.7 us
    scatter x2, local copies, waits for them, and re-layouts, pack_slots(): jnp.zeros((peers, slots, columns, width), jnp.bfloat16).at[dests, ranks]  18.7 us
    dot_general x2, matrix products, apply_local(): jnp.einsum('skl,slm->skm', inputs, operators, preferred_element_type=jnp....  18.3 us
    all_to_all x1, starting transfers between devices, per_device(): lax.all_to_all(id_slots, 'sub', split_axis=0, concat_axis=0, tiled=True)  8.59 us
  transfers between devices with their start and end apart: 2, of which 1 were waited for; matrix products, arithmetic and copies ran while one was open for 6% of the time, Pallas kernels for 0%

commit v1 on v0

--- a/solution.py
+++ b/solution.py
@@ -65,7 +65,7 @@
     )
     dual = accumulate(received, got_ids, own_blocks, weight)
     coeff = jnp.dot(dual.astype(jnp.bfloat16), basis, preferred_element_type=jnp.float32)
-    summed = lax.psum(coeff, "sub")
+    summed = jnp.sum(lax.all_gather(coeff, "sub"), axis=0)
     solved = jnp.dot(
         summed.astype(jnp.bfloat16), coarse, preferred_element_type=jnp.float32
     ).astype(jnp.bfloat16)

time: 338 us -> 282 us (0.83)
  blocking collectives: 192 us -> 65.8 us
  waiting for transfers between devices: 26.7 us -> 78.5 us
  between operations: 0.79 us -> 14.2 us
    psum x1 -> x0, blocking collectives: 121 us -> none  [per_device(): summed = lax.psum(coeff, 'sub')]
    all_gather x0 -> x1, waiting for transfers between devices: none -> 51.5 us  [per_device(): summed = jnp.sum(lax.all_gather(coeff, 'sub'), axis=0)]
    all_to_all x1, blocking collectives: 38.3 us -> 33.7 us  [per_device(): lax.all_to_all(requested, 'sub', split_axis=0, concat_axis=0, tiled=True)]
    reduce_sum x0 -> x1, other arithmetic: none -> 4.01 us  [per_device(): summed = jnp.sum(lax.all_gather(coeff, 'sub'), axis=0)]
  transfers between devices with their start and end apart: 2 -> 3, of which waited for: 1 -> 2; matrix products, arithmetic and copies ran while one was open for 6% -> 8% of each run, Pallas kernels for 0% -> 0%
where the time goes in v1:
time: 282 us; the launch traced here: 280 us
  waiting for transfers between devices  78.5 us (28%)
  blocking collectives  65.8 us (23%)
  other arithmetic  40.9 us (15%)
  local copies, waits for them, and re-layouts  38.8 us (14%)
  matrix products  26 us (9%)
  starting transfers between devices  16.1 us (6%)
  between operations  14.2 us (5%)
    all_gather x1, waiting for transfers between devices, per_device(): summed = jnp.sum(lax.all_gather(coeff, 'sub'), axis=0)  51.5 us
    all_to_all x1, blocking collectives, per_device(): lax.all_to_all(requested, 'sub', split_axis=0, concat_axis=0, tiled=True)  33.7 us
    all_to_all x1, blocking collectives, per_device(): lax.all_to_all(pack_slots(make_blocks(again, width), dests, ranks, peers,...  32.1 us
    scatter-add x2, other arithmetic, accumulate(): jnp.zeros((own_blocks, columns, width), jnp.float32).at[got_ids.reshape(-1)]  27.1 us
    all_to_all x1, waiting for transfers between devices, per_device(): lax.all_to_all(packed, 'sub', split_axis=0, concat_axis=0, tiled=True)  27 us
    scatter x2, local copies, waits for them, and re-layouts, pack_slots(): jnp.zeros((peers, slots, columns, width), jnp.bfloat16).at[dests, ranks]  19.6 us
    dot_general x2, matrix products, apply_local(): jnp.einsum('skl,slm->skm', inputs, operators, preferred_element_type=jnp....  18.3 us
    all_to_all x1, starting transfers between devices, per_device(): lax.all_to_all(id_slots, 'sub', split_axis=0, concat_axis=0, tiled=True)  8.59 us
  transfers between devices with their start and end apart: 3, of which 2 were waited for; matrix products, arithmetic and copies ran while one was open for 8% of the time, Pallas kernels for 0%

profile of v1, /device:TPU:1, one launch (start us, length us, event | category | flops | bytes accessed | tf_op | source)
XLA Modules:
  0.0 280.2 jit_solution(17387380930353697383)
XLA Ops:
  7.2 1.0 convert_reduce_fusion
  8.2 0.7 fusion.15
  8.9 5.7 %scatter_fusion = s32[32,4]{0,1:T(4,128)S(1)} fusion(s32[32,4]{0,1:T(4,128)S(1)} %broadcast.75, s32[64]{0:T(128)S(1)} %get-tuple-element.2, s32[64]{0:T(128)} %param.10), kind=kCustom, calls=%fused_computation.2 | custom fusion | bytes 1280 | tf_op jit(solution)/shard_map/scatter | solution.py:61
  14.6 0.7 copy.33
  15.3 8.6 %all-to-all-start = ((s32[32,1,4]{2,1,0:T(1,128)}), s32[32,1,4]{2,1,0:T(1,128)S(1)}, u32[]{:S(2)}, u32[]{:S(2)}) async-start(s32[32,1,4]{2,1,0:T(1,128)} %copy.33), calls=%async_computation | async-start | bytes 32768 | tf_op jit(solution)/shard_map/all_to_all | solution.py:64
  23.9 9.1 %fusion = bf16[8,8,8,8,128]{4,3,2,1,0:T(8,128)(2,1)S(1)} fusion(bf16[8,64,1024]{2,1,0:T(8,128)(2,1)} %param.7, bf16[8,1024,1024]{2,1,0:T(8,128)(2,1)} %param.8), kind=kOutput, calls=%fused_computation.11 | convolution fusion | flops 1074266112 | bytes 18874368 | tf_op jit(solution)/shard_map/skl,slm->skm/dot_general | solution.py:10
  33.0 1.3 copy.63
  34.3 1.9 broadcast.81.clone
  36.2 9.8 %scatter_fusion.1 = bf16[32,4,64,128]{3,2,1,0:T(8,128)(2,1)} fusion(bf16[32,4,64,128]{3,2,1,0:T(8,128)(2,1)} %broadcast.81.clone, s32[64]{0:T(128)S(1)} %get-tuple-element.2, bf16[64,64,128]{2,1,0:T(8,128)(2,1)} %bitcast.89), kind=kCustom, calls=%fused_computation.3 | custom fusion | bytes 3146240 | tf_op jit(solution)/shard_map/scatter | solution.py:36
  46.0 7.5 %all-to-all-start.1 = ((bf16[32,4,64,128]{3,2,1,0:T(8,128)(2,1)}), bf16[32,4,64,128]{3,2,1,0:T(8,128)(2,1)}, u32[]{:S(2)}, u32[]{:S(2)}) async-start(bf16[32,4,64,128]{3,2,1,0:T(8,128)(2,1)} %scatter_fusion.1), calls=%async_computation.1 | async-start | bytes 4194304 | tf_op jit(solution)/shard_map/all_to_all | solution.py:63
  53.5 0.5 broadcast.184
  54.0 0.7 reduce.3
  54.7 0.1 reshape.115
  54.9 27.0 %all-to-all-done.1 = bf16[32,4,64,128]{3,2,1,0:T(8,128)(2,1)} async-done(((bf16[32,4,64,128]{3,2,1,0:T(8,128)(2,1)}), bf16[32,4,64,128]{3,2,1,0:T(8,128)(2,1)}, u32[]{:S(2)}, u32[]{:S(2)}) %all-to-all-start.1) | async-done | bytes 2097184 | tf_op jit(solution)/shard_map/all_to_all | solution.py:63
  81.8 4.0 %bitcast_convert_fusion.1 = f32[128,64,128]{2,1,0:T(8,128)} fusion(bf16[32,4,64,128]{3,2,1,0:T(8,128)(2,1)} %all-to-all-done.1), kind=kLoop, calls=%fused_computation.8 | loop fusion | flops 1048576 | bytes 6291456 | tf_op jit(solution)/shard_map/convert_element_type | solution.py:41
  85.8 13.5 %scatter_fusion.2 = f32[16,64,128]{2,1,0:T(8,128)S(1)} fusion(f32[16,64,128]{2,1,0:T(8,128)S(1)} %broadcast.74.clone, s32[128]{0:T(128)S(1)} %fusion.14, f32[128,64,128]{2,1,0:T(8,128)} %bitcast_convert_fusion.1), kind=kCustom, calls=%fused_computation.4 | custom fusion | flops 1048576 | bytes 12583424 | tf_op jit(solution)/shard_map/scatter-add | solution.py:42
  99.4 3.8 %fusion.7 = f32[64,1024]{1,0:T(8,128)} fusion(bf16[2048,1024]{1,0:T(8,128)(2,1)} %param.12, f32[2048]{0:T(1024)S(1)} %add_divide_fusion, f32[16,64,128]{2,1,0:T(8,128)S(1)} %scatter_fusion.2), kind=kOutput, calls=%fused_computation.23 | convolution fusion | flops 268697600 | bytes 4988928 | tf_op jit(solution)/shard_map/dot_general | solution.py:67
  103.3 0.1 reshape.129
  103.5 51.5 %all-gather.3.cloned.1.call-done = f32[2048,1024]{1,0:T(8,128)} async-done(((f32[64,1024]{1,0:T(8,128)}), f32[2048,1024]{1,0:T(8,128)}) %all-gather.3.cloned.1.call-update) | async-done | bytes 8388624 | tf_op jit(solution)/shard_map/all_gather | solution.py:68
  155.0 4.0 %reduce_sum.22 = bf16[64,1024]{1,0:T(8,128)(2,1)S(1)} reduce(f32[32,64,1024]{2,1,0:T(8,128)} %bitcast.86, f32[]{:T(128)} %constant.7.clone.1), dimensions={0}, to_apply=%region_4.0 | reduce | flops 2031616 | bytes 8519684 | tf_op jit(solution)/shard_map/reduce_sum | solution.py:68
  159.0 3.9 %fusion.2 = f32[64,2048]{1,0:T(8,128)S(1)} fusion(bf16[2048,1024]{1,0:T(8,128)(2,1)} %param.12, bf16[1024,1024]{1,0:T(8,128)(2,1)S(1)} %copy-done, bf16[64,1024]{1,0:T(8,128)(2,1)S(1)} %reduce_sum.22), kind=kOutput, calls=%fused_computation.14 | convolution fusion | flops 402718720 | bytes 6946816 | tf_op jit(solution)/shard_map/dot_general | solution.py:72
  163.0 2.1 gather_fusion
  165.1 33.7 %all_to_all.27 = bf16[32,4,64,128]{3,2,1,0:T(8,128)(2,1)} all-to-all(bf16[32,4,64,128]{3,2,1,0:T(8,128)(2,1)} %bitcast.87), channel_id=1, replica_groups=mesh['sub'=32,'rep'=4] {'sub'}, dimensions={0} | all-to-all | bytes 4194304 | tf_op jit(solution)/shard_map/all_to_all | solution.py:78
  198.9 3.3 %gather_fusion.1 = bf16[64,64,128]{2,1,0:T(8,128)(2,1)} fusion(bf16[32,4,64,128]{3,2,1,0:T(8,128)(2,1)} %all_to_all.27, s32[64]{0:T(128)S(1)} %bitcast.91), kind=kCustom, calls=%fused_computation.1 | custom fusion | bytes 2097664 | tf_op jit(solution)/shard_map/gather | solution.py:79
  202.2 9.1 %fusion.1 = bf16[8,8,8,8,128]{4,3,2,1,0:T(8,128)(2,1)S(1)} fusion(bf16[8,1024,1024]{2,1,0:T(8,128)(2,1)} %param.8, bf16[8,8,8,8,128]{4,3,2,1,0:T(8,128)(2,1)} %bitcast.90), kind=kOutput, calls=%fused_computation.12 | convolution fusion | flops 1074266112 | bytes 18874368 | tf_op jit(solution)/shard_map/skl,slm->skm/dot_general | solution.py:10
  211.3 1.3 copy.62
  212.6 1.9 broadcast.81
  214.5 9.8 %scatter_fusion.3 = bf16[32,4,64,128]{3,2,1,0:T(8,128)(2,1)} fusion(bf16[32,4,64,128]{3,2,1,0:T(8,128)(2,1)} %broadcast.81, s32[64]{0:T(128)S(1)} %get-tuple-element.2, bf16[64,64,128]{2,1,0:T(8,128)(2,1)} %bitcast.88), kind=kCustom, calls=%fused_computation.5 | custom fusion | bytes 3146240 | tf_op jit(solution)/shard_map/scatter | solution.py:36
  224.3 32.1 %all_to_all.28 = bf16[32,4,64,128]{3,2,1,0:T(8,128)(2,1)S(1)} all-to-all(bf16[32,4,64,128]{3,2,1,0:T(8,128)(2,1)} %scatter_fusion.3), channel_id=1, replica_groups=mesh['sub'=32,'rep'=4] {'sub'}, dimensions={0} | all-to-all | bytes 4194304 | tf_op jit(solution)/shard_map/all_to_all | solution.py:82
  256.4 2.5 bitcast_convert_fusion
  259.0 13.5 %scatter_fusion.4 = f32[16,64,128]{2,1,0:T(8,128)S(1)} fusion(f32[16,64,128]{2,1,0:T(8,128)S(1)} %broadcast.74, s32[128]{0:T(128)S(1)} %fusion.14, f32[128,64,128]{2,1,0:T(8,128)} %bitcast_convert_fusion), kind=kCustom, calls=%fused_computation.6 | custom fusion | flops 1048576 | bytes 12583424 | tf_op jit(solution)/shard_map/scatter-add | solution.py:42
  272.5 0.9 fusion.5
  (19 shorter events, 0.4 us)
Async XLA Ops:
  7.2 151.8 %copy-start = (bf16[1024,1024]{1,0:T(8,128)(2,1)S(1)}, bf16[1024,1024]{1,0:T(8,128)(2,1)}, u32[]{:S(2)}) copy-start(bf16[1024,1024]{1,0:T(8,128)(2,1)} %param.13) | copy-start | bytes 6291460
  15.3 30.7 %all-to-all-start = ((s32[32,1,4]{2,1,0:T(1,128)}), s32[32,1,4]{2,1,0:T(1,128)S(1)}, u32[]{:S(2)}, u32[]{:S(2)}) async-start(s32[32,1,4]{2,1,0:T(1,128)} %copy.33), calls=%async_computation | async-start | bytes 32768 | tf_op jit(solution)/shard_map/all_to_all | solution.py:64
  36.2 17.3 %copy-start.2 = (s32[2048]{0:T(1024)S(1)}, s32[2048]{0:T(1024)}, u32[]{:S(2)}) copy-start(s32[2048]{0:T(1024)} %param.11) | copy-start | bytes 24580
  46.0 35.8 %all-to-all-start.1 = ((bf16[32,4,64,128]{3,2,1,0:T(8,128)(2,1)}), bf16[32,4,64,128]{3,2,1,0:T(8,128)(2,1)}, u32[]{:S(2)}, u32[]{:S(2)}) async-start(bf16[32,4,64,128]{3,2,1,0:T(8,128)(2,1)} %scatter_fusion.1), calls=%async_computation.1 | async-start | bytes 4194304 | tf_op jit(solution)/shard_map/all_to_all | solution.py:63
  53.5 101.5 %all-gather.3.cloned.1.call-start = ((), (), s32[]{:S(2)}) async-start(), calls=%async_computation.4 | async-start | bytes 8650752 | tf_op jit(solution)/shard_map/all_gather | solution.py:68
  163.0 35.9 %copy-start.1 = (f32[64,2048]{1,0:T(8,128)}, f32[64,2048]{1,0:T(8,128)S(1)}, u32[]{:S(2)}) copy-start(f32[64,2048]{1,0:T(8,128)S(1)} %fusion.2) | copy-start | bytes 1572868
Sparse Core Ops, SparseCore 0:
  103.3 51.6 all-gather.2
